TPU v7x, 512 devices: a whole 4x8x8 slice. The times are simulated.
512 devices in a mesh: pair: 64 (over z, x, core), slab: 8 (over y).
Axes of the slice: x: 4, y: 8, z: 8, core: 2. Of those that a mesh axis runs over, the one named last changes fastest.
Arguments:
- amps: bfloat16 [1024, 1024, 128], P(('pair', 'slab')), may hold values from -6 to 6
- symmetry: int32 [1024], replicated, may hold values from 0 to 3
- screen: int32 [64, 16, 16], P('pair'), may hold values 0 or 1
- owner: int32 [1024], replicated, may hold values from 0 to 63, as said below
- integrals: bfloat16 [64, 2048, 2048], P('pair', 'slab'), may hold values from -0.25 to 0.25
Outputs:
- residual: bfloat16 [1024, 64, 16, 128], P(('pair', 'slab'))
Inputs may be any that keep to these rules, and one draw needn't show every extreme that they name: Every owner from 0 to 63 holds exactly 16 tiles.
All inputs are finite; a program needn't handle non-finite values. No bound on the sum of `screen` on one device may be relied on, other than what follows from the above.
Results may differ from a plain program's by a relative error of at most 0.001.
Values may be sent and summed in bfloat16 or wider, within the bound.
A program may use at most 64 MiB of HBM per device.

v0:
```python
import jax
import jax.numpy as jnp
from jax import lax
from jax.sharding import PartitionSpec as P


def contract(operand, block_piece, mask_piece, per_owner, tile_width):
    rows_here = block_piece.shape[0]
    masked = (
        block_piece.reshape(rows_here, per_owner, tile_width) * mask_piece[:, :, None]
    ).reshape(rows_here, per_owner * tile_width)
    return jnp.dot(operand, masked, preferred_element_type=jnp.float32)


def on_device(amps, symmetry, screen, owner, integrals):
    n_pair = lax.axis_size("pair")
    local_rows, tile_count, tile_width = amps.shape
    per_owner = tile_count // n_pair
    owner_span = per_owner * tile_width
    tile_order = jnp.argsort(owner, stable=True).reshape(n_pair, per_owner)
    sorted_amps = jnp.take(amps, tile_order.reshape(-1), axis=1).reshape(
        local_rows, n_pair, owner_span
    )
    owned = lax.dynamic_index_in_dim(tile_order, lax.axis_index("pair"), 0, keepdims=False)
    labels = jnp.take(symmetry, owned)
    allowed = ((labels[:, None] == labels[None, :]) & (screen[0] == 1)).astype(jnp.bfloat16)
    mask_rows = jnp.repeat(allowed, tile_width, axis=0)
    block_rows = integrals[0]
    received = lax.all_to_all(sorted_amps, "pair", split_axis=1, concat_axis=1, tiled=True)
    flat_rows = received.reshape(local_rows * n_pair, owner_span)
    summed = contract(
        flat_rows,
        lax.all_gather(block_rows, "slab", axis=0, tiled=True),
        mask_rows,
        per_owner,
        tile_width,
    )
    product = summed.astype(jnp.bfloat16).reshape(local_rows, n_pair, owner_span)
    returned = lax.all_to_all(product, "pair", split_axis=1, concat_axis=1, tiled=True)
    return returned.reshape(local_rows, n_pair, per_owner, tile_width)


def solution(mesh):
    in_specs = (
        P(("pair", "slab"), None, None),
        P(),
        P("pair", None, None),
        P(),
        P("pair", "slab", None),
    )
    out_specs = P(("pair", "slab"), None, None, None)
    return jax.shard_map(
        on_device, mesh=mesh, in_specs=in_specs, out_specs=out_specs, check_vma=False
    )
```

profile of v0, /device:TPU:1, one launch (start us, length us, event | category | flops | bytes accessed | tf_op | source)
XLA Modules:
  0.0 163.3 jit_solution(9701086411608174818)
XLA Ops:
  6.5 0.0 copy-start
  6.5 0.0 copy-start.1
  6.5 0.0 copy-start.2
  6.5 0.0 all-gather.3.cloned.1.call-start
  6.5 0.7 all-gather.3.cloned.1.call-update
  7.3 5.1 %sort.17 = (s32[1024]{0:T(1024)}, s32[1024]{0:T(1024)S(1)}) sort(s32[1024]{0:T(1024)} %param.8, s32[1024]{0:T(1024)S(1)} %iota.4), dimensions={0}, to_apply=%region_0.0 | sort | flops 10240 | bytes 16384 | tf_op jit(solution)/shard_map/jit(argsort)/sort | solution.py:20
  12.3 0.1 broadcast_in_dim.25
  12.4 0.2 broadcast_in_dim.26
  12.6 0.1 copy.23
  12.7 0.0 copy-done
  12.7 4.4 %gather_fusion = bf16[1024,2,128]{2,0,1:T(8,128)(2,1)S(1)} fusion(bf16[2,1024,128]{2,1,0:T(8,128)(2,1)S(1)} %copy-done, s32[1024]{0:T(1024)S(1)} %fusion.5), kind=kCustom, calls=%fused_computation | custom fusion | bytes 1052672 | tf_op jit(solution)/shard_map/jit(_take)/gather | solution.py:21
  17.1 0.2 gather.13
  17.4 1.9 %broadcast_select_fusion = bf16[2,64,2048]{2,0,1:T(2,128)(2,1)} fusion(pred[64,2048]{1,0:T(8,128)(4,1)S(1)} %bitcast.43, bf16[2,64,2048]{2,1,0:T(8,128)(2,1)S(1)} %gather.13), kind=kLoop, calls=%fused_computation.7 | loop fusion | flops 262144 | bytes 1179648 | tf_op jit(solution)/shard_map/jit(_take)/select_n | solution.py:21
  19.2 14.8 %all-to-all-start = ((bf16[2,64,2048]{2,0,1:T(2,128)(2,1)}), bf16[2,64,2048]{2,0,1:T(2,128)(2,1)S(1)}, u32[]{:S(2)}, u32[]{:S(2)}) async-start(bf16[2,64,2048]{2,0,1:T(2,128)(2,1)} %broadcast_select_fusion), calls=%async_computation | async-start | bytes 1048576 | tf_op jit(solution)/shard_map/all_to_all | solution.py:29
  34.1 0.1 reshape.78
  34.2 0.0 copy-done.1
  34.2 0.6 gather_fusion.1
  34.9 0.0 copy-done.2
  34.9 0.1 fusion.4
  35.0 16.8 %all-to-all-done = bf16[2,64,2048]{2,0,1:T(2,128)(2,1)S(1)} async-done(((bf16[2,64,2048]{2,0,1:T(2,128)(2,1)}), bf16[2,64,2048]{2,0,1:T(2,128)(2,1)S(1)}, u32[]{:S(2)}, u32[]{:S(2)}) %all-to-all-start) | async-done | bytes 524320 | tf_op jit(solution)/shard_map/all_to_all | solution.py:29
  51.8 0.2 copy.10
  52.0 59.5 %all-gather.3.cloned.1.call-done = bf16[1,2048,2048]{2,1,0:T(8,128)(2,1)} async-done(((bf16[1,256,2048]{2,1,0:T(8,128)(2,1)}), bf16[1,2048,2048]{2,1,0:T(8,128)(2,1)}) %all-gather.3.cloned.1.call-update) | async-done | bytes 8388624 | tf_op jit(solution)/shard_map/all_gather | solution.py:33
  111.5 0.0 copy-start.3
  111.5 0.1 broadcast_in_dim.31
  111.5 9.0 %mul.14 = bf16[2048,16,128]{2,1,0:T(8,128)(2,1)S(1)} broadcast(bf16[2048,16]{1,0:T(8,128)(2,1)S(1)} %bitcast.41), dimensions={0,1} | broadcast | bytes 8454144 | tf_op jit(solution)/shard_map/mul | solution.py:10
  120.5 0.0 copy-done.3
  120.5 5.7 %fusion.3 = bf16[128,2048]{1,0:T(8,128)(2,1)S(1)} fusion(bf16[128,2048]{1,0:T(8,128)(2,1)S(1)} %bitcast.44, bf16[256,8,16,128]{3,2,1,0:T(8,128)(2,1)S(1)} %bitcast.40, bf16[1,2048,2048]{2,1,0:T(8,128)(2,1)S(1)} %copy-done.3), kind=kOutput, calls=%fused_computation.6 | convolution fusion | flops 1078198272 | bytes 17825792 | tf_op jit(solution)/shard_map/dot_general | solution.py:12
  126.2 0.5 copy.11
  126.7 28.5 %all_to_all.10 = bf16[2,64,2048]{2,0,1:T(2,128)(2,1)S(1)} all-to-all(bf16[2,64,2048]{2,0,1:T(2,128)(2,1)S(1)} %copy.11), channel_id=1, replica_groups=mesh['pair'=64,'slab'=8] {'pair'}, dimensions={1} | all-to-all | bytes 1048576 | tf_op jit(solution)/shard_map/all_to_all | solution.py:39
  155.3 0.3 reshape.80
  155.6 0.8 copy.12
  (7 shorter events, 0.1 us)
Async XLA Ops:
  6.5 6.2 %copy-start = (bf16[2,1024,128]{2,1,0:T(8,128)(2,1)S(1)}, bf16[2,1024,128]{2,1,0:T(8,128)(2,1)}, u32[]{:S(2)}) copy-start(bf16[2,1024,128]{2,1,0:T(8,128)(2,1)} %param.5) | copy-start | bytes 1572868
  6.5 27.7 %copy-start.1 = (s32[1024]{0:T(1024)S(1)}, s32[1024]{0:T(1024)}, u32[]{:S(2)}) copy-start(s32[1024]{0:T(1024)} %param.6) | copy-start | bytes 12292
  6.5 28.3 %copy-start.2 = (s32[1,16,16]{2,1,0:T(8,128)S(1)}, s32[1,16,16]{2,1,0:T(8,128)}, u32[]{:S(2)}) copy-start(s32[1,16,16]{2,1,0:T(8,128)} %param.7) | copy-start | bytes 3076
  6.5 104.9 %all-gather.3.cloned.1.call-start = ((), (), s32[]{:S(2)}) async-start(), calls=%async_computation.2 | async-start | bytes 9437184 | tf_op jit(solution)/shard_map/all_gather | solution.py:33
  19.2 32.6 %all-to-all-start = ((bf16[2,64,2048]{2,0,1:T(2,128)(2,1)}), bf16[2,64,2048]{2,0,1:T(2,128)(2,1)S(1)}, u32[]{:S(2)}, u32[]{:S(2)}) async-start(bf16[2,64,2048]{2,0,1:T(2,128)(2,1)} %broadcast_select_fusion), calls=%async_computation | async-start | bytes 1048576 | tf_op jit(solution)/shard_map/all_to_all | solution.py:29
  111.5 9.0 %copy-start.3 = (bf16[1,2048,2048]{2,1,0:T(8,128)(2,1)S(1)}, bf16[1,2048,2048]{2,1,0:T(8,128)(2,1)}, u32[]{:S(2)}) copy-start(bf16[1,2048,2048]{2,1,0:T(8,128)(2,1)} %all-gather.3.cloned.1.call-done) | copy-start | bytes 25165828
Sparse Core Ops, SparseCore 0:
  9.4 101.9 all-gather.2
where the time goes:
time: 164 us; the launch traced here: 163 us
  waiting for transfers between devices  77 us (47%)
  blocking collectives  28.5 us (17%)
  local copies, waits for them, and re-layouts  16.6 us (10%)
  starting transfers between devices  14.8 us (9%)
  between operations  13.6 us (8%)
  other arithmetic  7.06 us (4%)
  matrix products  5.67 us (3%)
    all_gather x1, waiting for transfers between devices, on_device(): lax.all_gather(block_rows, 'slab', axis=0, tiled=True)  59.5 us
    all_to_all x1, blocking collectives, on_device(): lax.all_to_all(product, 'pair', split_axis=1, concat_axis=1, tiled=True)  28.5 us
    all_to_all x1, waiting for transfers between devices, on_device(): lax.all_to_all(sorted_amps, 'pair', split_axis=1, concat_axis=1, tiled=True)  16.8 us
    all_to_all x1, starting transfers between devices, on_device(): lax.all_to_all(sorted_amps, 'pair', split_axis=1, concat_axis=1, tiled=True)  14.8 us
    mul x1, local copies, waits for them, and re-layouts, contract(): block_piece.reshape(rows_here, per_owner, tile_width)  8.96 us
    dot_general x1, matrix products, contract(): return jnp.dot(operand, masked, preferred_element_type=jnp.float32)  5.67 us
    sort x1, other arithmetic, on_device(): tile_order = jnp.argsort(owner, stable=True).reshape(n_pair, per_owner)  5.05 us
    gather x2, local copies, waits for them, and re-layouts, on_device(): jnp.take(amps, tile_order.reshape(-1), axis=1)  4.62 us
  transfers between devices with their start and end apart: 2, of which 2 were waited for; matrix products, arithmetic and copies ran while one was open for 8% of the time, Pallas kernels for 0%

commit v1 on v0

--- a/solution.py
+++ b/solution.py
@@ -28,13 +28,23 @@
     block_rows = integrals[0]
     received = lax.all_to_all(sorted_amps, "pair", split_axis=1, concat_axis=1, tiled=True)
     flat_rows = received.reshape(local_rows * n_pair, owner_span)
-    summed = contract(
-        flat_rows,
-        lax.all_gather(block_rows, "slab", axis=0, tiled=True),
-        mask_rows,
-        per_owner,
-        tile_width,
-    )
+
+    def turn_roads(own_rows, which_axis):
+        n_axis = lax.axis_size(which_axis)
+        line_up = [(no, (no + 1) % n_axis) for no in range(n_axis)]
+        samples = [(no, (no - 1) % n_axis) for no in range(n_axis)]
+        v1, left_arr = ([own_rows], [own_rows])
+        for _ in range(n_axis // 2):
+            v1.append(lax.ppermute(v1[-1], axis_name=which_axis, perm=line_up))
+        for _ in range((n_axis - 1) // 2):
+            mixed_arr = lax.ppermute(left_arr[-1], axis_name=which_axis, perm=samples)
+            left_arr.append(mixed_arr)
+        block_next = jnp.concatenate([*v1[::-1], *left_arr[1:]], 0)
+        return jnp.roll(
+            block_next, (lax.axis_index(which_axis) - n_axis // 2) * own_rows.shape[0], 0
+        )
+
+    summed = contract(flat_rows, turn_roads(block_rows, "slab"), mask_rows, per_owner, tile_width)
     product = summed.astype(jnp.bfloat16).reshape(local_rows, n_pair, owner_span)
     returned = lax.all_to_all(product, "pair", split_axis=1, concat_axis=1, tiled=True)
     return returned.reshape(local_rows, n_pair, per_owner, tile_width)

time: 164 us -> 196 us (1.20)
  starting transfers between devices: 14.8 us -> 48.6 us
  local copies, waits for them, and re-layouts: 16.6 us -> 36.3 us
  between operations: 13.6 us -> 0.32 us
  waiting for transfers between devices: 77 us -> 71.7 us
  blocking collectives: 28.5 us -> 23.7 us
    all_gather x1 -> x0, waiting for transfers between devices: 59.5 us -> none  [on_device(): lax.all_gather(block_rows, 'slab', axis=0, tiled=True)]
    ppermute x0 -> x7, waiting for transfers between devices: none -> 56.2 us  [the longest x4 40.4 us: turn_roads(): v1.append(lax.ppermute(v1[-1], axis_name=which_axis, perm=line_up))]
    ppermute x0 -> x7, starting transfers between devices: none -> 28 us  [the longest x4 14.4 us: turn_roads(): v1.append(lax.ppermute(v1[-1], axis_name=which_axis, perm=line_up))]
    unnamed x9 -> x20, local copies, waits for them, and re-layouts: 0.08 us -> 13.4 us
    all_to_all x1, starting transfers between devices: 14.8 us -> 20.6 us  [on_device(): lax.all_to_all(sorted_amps, 'pair', split_axis=1, concat_axis=1, tiled=True)]
    gather x2, local copies, waits for them, and re-layouts: 4.62 us -> 10.3 us  [on_device(): jnp.take(amps, tile_order.reshape(-1), axis=1)]
    all_to_all x1, blocking collectives: 28.5 us -> 23.7 us  [on_device(): lax.all_to_all(product, 'pair', split_axis=1, concat_axis=1, tiled=True)]
  transfers between devices with their start and end apart: 2 -> 8, of which waited for: 2 -> 5; matrix products, arithmetic and copies ran while one was open for 8% -> 14% of each run, Pallas kernels for 0% -> 0%
where the time goes in v1:
time: 196 us; the launch traced here: 194 us
  waiting for transfers between devices  71.7 us (37%)
  starting transfers between devices  48.6 us (25%)
  local copies, waits for them, and re-layouts  36.3 us (19%)
  blocking collectives  23.7 us (12%)
  other arithmetic  7.76 us (4%)
  matrix products  5.9 us (3%)
    ppermute x4, waiting for transfers between devices, turn_roads(): v1.append(lax.ppermute(v1[-1], axis_name=which_axis, perm=line_up))  40.4 us
    all_to_all x1, blocking collectives, on_device(): lax.all_to_all(product, 'pair', split_axis=1, concat_axis=1, tiled=True)  23.7 us
    all_to_all x1, starting transfers between devices, on_device(): lax.all_to_all(sorted_amps, 'pair', split_axis=1, concat_axis=1, tiled=True)  20.6 us
    ppermute x3, waiting for transfers between devices, turn_roads(): mixed_arr = lax.ppermute(left_arr[-1], axis_name=which_axis, perm=samples)  15.8 us
    all_to_all x1, waiting for transfers between devices, on_device(): lax.all_to_all(sorted_amps, 'pair', split_axis=1, concat_axis=1, tiled=True)  15.5 us
    ppermute x4, starting transfers between devices, turn_roads(): v1.append(lax.ppermute(v1[-1], axis_name=which_axis, perm=line_up))  14.4 us
    ppermute x3, starting transfers between devices, turn_roads(): mixed_arr = lax.ppermute(left_arr[-1], axis_name=which_axis, perm=samples)  13.6 us
    unnamed x20, local copies, waits for them, and re-layouts  13.4 us
  transfers between devices with their start and end apart: 8, of which 5 were waited for; matrix products, arithmetic and copies ran while one was open for 14% of the time, Pallas kernels for 0%

profile of v1, /device:TPU:1, one launch (start us, length us, event | category | flops | bytes accessed | tf_op | source)
XLA Modules:
  0.0 194.3 jit_solution(8331341670332986251)
XLA Ops:
  0.0 0.0 copy-start
  0.0 0.0 copy-start.1
  0.0 4.2 %collective-permute-start = (bf16[256,2048]{1,0:T(8,128)(2,1)}, bf16[256,2048]{1,0:T(8,128)(2,1)S(1)}, u32[]{:S(2)}, u32[]{:S(2)}) collective-permute-start(bf16[256,2048]{1,0:T(8,128)(2,1)} %bitcast.37), channel_id=1, source_target_pairs={{0,1},{1,2},{2,3},{3,4},{4,5},{5,6},{6,7},{7,0},{8,9},{9,10},{10,1... | collective-permute-start | bytes 3145736 | tf_op jit(solution)/shard_map/ppermute | solution.py:38
  4.2 19.8 %collective-permute-done = bf16[256,2048]{1,0:T(8,128)(2,1)S(1)} collective-permute-done((bf16[256,2048]{1,0:T(8,128)(2,1)}, bf16[256,2048]{1,0:T(8,128)(2,1)S(1)}, u32[]{:S(2)}, u32[]{:S(2)}) %collective-permute-start) | collective-permute-done | bytes 1048608 | tf_op jit(solution)/shard_map/ppermute | solution.py:38
  23.9 5.8 %collective-permute-start.1 = (bf16[256,2048]{1,0:T(8,128)(2,1)S(1)}, bf16[256,2048]{1,0:T(8,128)(2,1)}, u32[]{:S(2)}, u32[]{:S(2)}) collective-permute-start(bf16[256,2048]{1,0:T(8,128)(2,1)S(1)} %collective-permute-done), channel_id=1, source_target_pairs={{0,1},{1,2},{2,3},{3,4},{4,5},{5,6},{6,7},{7,0},{8,9},{9,10},{10,1... | collective-permute-start | bytes 3145736 | tf_op jit(solution)/shard_map/ppermute | solution.py:38
  29.8 4.3 %collective-permute-start.4 = (bf16[256,2048]{1,0:T(8,128)(2,1)}, bf16[256,2048]{1,0:T(8,128)(2,1)}, u32[]{:S(2)}, u32[]{:S(2)}) collective-permute-start(bf16[256,2048]{1,0:T(8,128)(2,1)} %bitcast.38), channel_id=1, source_target_pairs={{0,7},{1,0},{2,1},{3,2},{4,3},{5,4},{6,5},{7,6},{8,15},{9,8},{10,9... | collective-permute-start | bytes 3145736 | tf_op jit(solution)/shard_map/ppermute | solution.py:40
  34.1 18.6 %collective-permute-done.1 = bf16[256,2048]{1,0:T(8,128)(2,1)} collective-permute-done((bf16[256,2048]{1,0:T(8,128)(2,1)S(1)}, bf16[256,2048]{1,0:T(8,128)(2,1)}, u32[]{:S(2)}, u32[]{:S(2)}) %collective-permute-start.1) | collective-permute-done | bytes 1048608 | tf_op jit(solution)/shard_map/ppermute | solution.py:38
  52.7 2.1 %collective-permute-start.2 = (bf16[256,2048]{1,0:T(8,128)(2,1)}, bf16[256,2048]{1,0:T(8,128)(2,1)}, u32[]{:S(2)}, u32[]{:S(2)}) collective-permute-start(bf16[256,2048]{1,0:T(8,128)(2,1)} %collective-permute-done.1), channel_id=1, source_target_pairs={{0,1},{1,2},{2,3},{3,4},{4,5},{5,6},{6,7},{7,0},{8,9},{9,10},{10,1... | collective-permute-start | bytes 3145736 | tf_op jit(solution)/shard_map/ppermute | solution.py:38
  54.8 5.1 %sort.17 = (s32[1024]{0:T(1024)}, s32[1024]{0:T(1024)S(1)}) sort(s32[1024]{0:T(1024)} %param.8, s32[1024]{0:T(1024)S(1)} %iota.4), dimensions={0}, to_apply=%region_0.0 | sort | flops 10240 | bytes 16384 | tf_op jit(solution)/shard_map/jit(argsort)/sort | solution.py:20
  59.9 0.1 reshape.78
  60.0 0.0 copy-done
  60.0 9.0 %gather_fusion = bf16[1024,2,128]{2,0,1:T(8,128)(2,1)} fusion(bf16[2,1024,128]{2,1,0:T(8,128)(2,1)S(1)} %copy-done, s32[1024]{0:T(1024)S(1)} %get-tuple-element.8), kind=kCustom, calls=%fused_computation | custom fusion | bytes 1052672 | tf_op jit(solution)/shard_map/jit(_take)/gather | solution.py:21
  69.0 1.3 gather.13
  70.2 0.1 broadcast_in_dim.25
  70.3 0.2 broadcast_in_dim.26
  70.5 0.1 copy.23
  70.6 0.0 collective-permute-done.4
  70.6 4.4 %collective-permute-start.5 = (bf16[256,2048]{1,0:T(8,128)(2,1)}, bf16[256,2048]{1,0:T(8,128)(2,1)}, u32[]{:S(2)}, u32[]{:S(2)}) collective-permute-start(bf16[256,2048]{1,0:T(8,128)(2,1)} %collective-permute-done.4), channel_id=1, source_target_pairs={{0,7},{1,0},{2,1},{3,2},{4,3},{5,4},{6,5},{7,6},{8,15},{9,8},{10,9... | collective-permute-start | bytes 3145736 | tf_op jit(solution)/shard_map/ppermute | solution.py:40
  75.0 2.0 %collective-permute-done.2 = bf16[256,2048]{1,0:T(8,128)(2,1)} collective-permute-done((bf16[256,2048]{1,0:T(8,128)(2,1)}, bf16[256,2048]{1,0:T(8,128)(2,1)}, u32[]{:S(2)}, u32[]{:S(2)}) %collective-permute-start.2) | collective-permute-done | bytes 1048608 | tf_op jit(solution)/shard_map/ppermute | solution.py:38
  77.1 2.3 %collective-permute-start.3 = (bf16[256,2048]{1,0:T(8,128)(2,1)}, bf16[256,2048]{1,0:T(8,128)(2,1)}, u32[]{:S(2)}, u32[]{:S(2)}) collective-permute-start(bf16[256,2048]{1,0:T(8,128)(2,1)} %collective-permute-done.2), channel_id=1, source_target_pairs={{0,1},{1,2},{2,3},{3,4},{4,5},{5,6},{6,7},{7,0},{8,9},{9,10},{10,1... | collective-permute-start | bytes 3145736 | tf_op jit(solution)/shard_map/ppermute | solution.py:38
  79.4 1.9 broadcast_select_fusion
  81.3 20.6 %all-to-all-start = ((bf16[2,64,2048]{2,0,1:T(2,128)(2,1)}), bf16[2,64,2048]{2,0,1:T(2,128)(2,1)S(1)}, u32[]{:S(2)}, u32[]{:S(2)}) async-start(bf16[2,64,2048]{2,0,1:T(2,128)(2,1)} %broadcast_select_fusion), calls=%async_computation | async-start | bytes 1048576 | tf_op jit(solution)/shard_map/all_to_all | solution.py:29
  101.9 1.3 gather_fusion.1
  103.3 0.8 fusion.4
  104.1 15.5 %all-to-all-done = bf16[2,64,2048]{2,0,1:T(2,128)(2,1)S(1)} async-done(((bf16[2,64,2048]{2,0,1:T(2,128)(2,1)}), bf16[2,64,2048]{2,0,1:T(2,128)(2,1)S(1)}, u32[]{:S(2)}, u32[]{:S(2)}) %all-to-all-start) | async-done | bytes 524320 | tf_op jit(solution)/shard_map/all_to_all | solution.py:29
  119.6 0.2 copy.10
  119.8 0.0 collective-permute-done.5
  119.8 4.9 %collective-permute-start.6 = (bf16[256,2048]{1,0:T(8,128)(2,1)}, bf16[256,2048]{1,0:T(8,128)(2,1)S(1)}, u32[]{:S(2)}, u32[]{:S(2)}) collective-permute-start(bf16[256,2048]{1,0:T(8,128)(2,1)} %collective-permute-done.5), channel_id=1, source_target_pairs={{0,7},{1,0},{2,1},{3,2},{4,3},{5,4},{6,5},{7,6},{8,15},{9,8},{10,9... | collective-permute-start | bytes 3145736 | tf_op jit(solution)/shard_map/ppermute | solution.py:40
  124.6 0.0 collective-permute-done.3
  124.6 1.3 constant_dynamic-update-slice_fusion.15
  125.9 1.3 constant_dynamic-update-slice_fusion.14
  127.2 1.3 constant_dynamic-update-slice_fusion.13
  128.5 0.1 constant_dynamic-update-slice_fusion.12
  128.6 0.0 copy-done.1
  128.6 0.1 constant_dynamic-update-slice_fusion.11
  128.7 1.3 constant_dynamic-update-slice_fusion.10
  130.0 1.3 constant_dynamic-update-slice_fusion.9
  131.3 15.8 %collective-permute-done.6 = bf16[256,2048]{1,0:T(8,128)(2,1)S(1)} collective-permute-done((bf16[256,2048]{1,0:T(8,128)(2,1)}, bf16[256,2048]{1,0:T(8,128)(2,1)S(1)}, u32[]{:S(2)}, u32[]{:S(2)}) %collective-permute-start.6) | collective-permute-done | bytes 1048608 | tf_op jit(solution)/shard_map/ppermute | solution.py:40
  147.1 0.1 constant_dynamic-update-slice_fusion.8
  147.2 1.3 constant_dynamic-update-slice_fusion.7
  148.5 1.3 constant_dynamic-update-slice_fusion.6
  149.8 1.3 constant_dynamic-update-slice_fusion.5
  151.1 0.1 constant_dynamic-update-slice_fusion.4
  151.2 0.1 constant_dynamic-update-slice_fusion.3
  151.2 1.3 constant_dynamic-update-slice_fusion.2
  152.5 1.3 constant_dynamic-update-slice_fusion.1
  153.8 0.1 constant_dynamic-update-slice_fusion
  153.9 0.1 broadcast_in_dim.31
  154.0 9.0 %mul.18 = bf16[2048,16,128]{2,1,0:T(8,128)(2,1)S(1)} broadcast(bf16[2048,16]{1,0:T(8,128)(2,1)S(1)} %bitcast.39), dimensions={0,1} | broadcast | bytes 8454144 | tf_op jit(solution)/shard_map/mul | solution.py:10
  163.0 5.9 %fusion.3 = bf16[128,2048]{1,0:T(8,128)(2,1)S(1)} fusion(bf16[128,2048]{1,0:T(8,128)(2,1)S(1)} %bitcast.42, bf16[256,8,16,128]{3,2,1,0:T(8,128)(2,1)S(1)} %bitcast.36, bf16[4096,2048]{1,0:T(8,128)(2,1)S(1)} %constant_dynamic-update-slice_fusion, s32[]{:T(128)S(6)} %select_n.63), kind=kOutput, calls=%fused_computation.6 | convolution fusion | flops 1090781184 | bytes 17825796 | tf_op jit(solution)/shard_map/dot_general | solution.py:12
  168.9 0.5 copy.11
  169.4 23.7 %all_to_all.10 = bf16[2,64,2048]{2,0,1:T(2,128)(2,1)S(1)} all-to-all(bf16[2,64,2048]{2,0,1:T(2,128)(2,1)S(1)} %copy.11), channel_id=1, replica_groups=mesh['pair'=64,'slab'=8] {'pair'}, dimensions={1} | all-to-all | bytes 1048576 | tf_op jit(solution)/shard_map/all_to_all | solution.py:49
  193.1 0.3 reshape.80
  193.5 0.8 copy.12
  (6 shorter events, 0.1 us)
Async XLA Ops:
  0.0 60.0 %copy-start = (bf16[2,1024,128]{2,1,0:T(8,128)(2,1)S(1)}, bf16[2,1024,128]{2,1,0:T(8,128)(2,1)}, u32[]{:S(2)}) copy-start(bf16[2,1024,128]{2,1,0:T(8,128)(2,1)} %param.5) | copy-start | bytes 1572868
  0.0 128.6 %copy-start.1 = (bf16[1,256,2048]{2,1,0:T(8,128)(2,1)S(1)}, bf16[1,256,2048]{2,1,0:T(8,128)(2,1)}, u32[]{:S(2)}) copy-start(bf16[1,256,2048]{2,1,0:T(8,128)(2,1)} %param.9) | copy-start | bytes 3145732
  0.0 23.9 %collective-permute-start = (bf16[256,2048]{1,0:T(8,128)(2,1)}, bf16[256,2048]{1,0:T(8,128)(2,1)S(1)}, u32[]{:S(2)}, u32[]{:S(2)}) collective-permute-start(bf16[256,2048]{1,0:T(8,128)(2,1)} %bitcast.37), channel_id=1, source_target_pairs={{0,1},{1,2},{2,3},{3,4},{4,5},{5,6},{6,7},{7,0},{8,9},{9,10},{10,1... | collective-permute-start | bytes 3145736 | tf_op jit(solution)/shard_map/ppermute | solution.py:38
  23.9 28.8 %collective-permute-start.1 = (bf16[256,2048]{1,0:T(8,128)(2,1)S(1)}, bf16[256,2048]{1,0:T(8,128)(2,1)}, u32[]{:S(2)}, u32[]{:S(2)}) collective-permute-start(bf16[256,2048]{1,0:T(8,128)(2,1)S(1)} %collective-permute-done), channel_id=1, source_target_pairs={{0,1},{1,2},{2,3},{3,4},{4,5},{5,6},{6,7},{7,0},{8,9},{9,10},{10,1... | collective-permute-start | bytes 3145736 | tf_op jit(solution)/shard_map/ppermute | solution.py:38
  29.8 40.8 %collective-permute-start.4 = (bf16[256,2048]{1,0:T(8,128)(2,1)}, bf16[256,2048]{1,0:T(8,128)(2,1)}, u32[]{:S(2)}, u32[]{:S(2)}) collective-permute-start(bf16[256,2048]{1,0:T(8,128)(2,1)} %bitcast.38), channel_id=1, source_target_pairs={{0,7},{1,0},{2,1},{3,2},{4,3},{5,4},{6,5},{7,6},{8,15},{9,8},{10,9... | collective-permute-start | bytes 3145736 | tf_op jit(solution)/shard_map/ppermute | solution.py:40
  52.7 24.4 %collective-permute-start.2 = (bf16[256,2048]{1,0:T(8,128)(2,1)}, bf16[256,2048]{1,0:T(8,128)(2,1)}, u32[]{:S(2)}, u32[]{:S(2)}) collective-permute-start(bf16[256,2048]{1,0:T(8,128)(2,1)} %collective-permute-done.1), channel_id=1, source_target_pairs={{0,1},{1,2},{2,3},{3,4},{4,5},{5,6},{6,7},{7,0},{8,9},{9,10},{10,1... | collective-permute-start | bytes 3145736 | tf_op jit(solution)/shard_map/ppermute | solution.py:38
  70.6 49.1 %collective-permute-start.5 = (bf16[256,2048]{1,0:T(8,128)(2,1)}, bf16[256,2048]{1,0:T(8,128)(2,1)}, u32[]{:S(2)}, u32[]{:S(2)}) collective-permute-start(bf16[256,2048]{1,0:T(8,128)(2,1)} %collective-permute-done.4), channel_id=1, source_target_pairs={{0,7},{1,0},{2,1},{3,2},{4,3},{5,4},{6,5},{7,6},{8,15},{9,8},{10,9... | collective-permute-start | bytes 3145736 | tf_op jit(solution)/shard_map/ppermute | solution.py:40
  77.1 47.5 %collective-permute-start.3 = (bf16[256,2048]{1,0:T(8,128)(2,1)}, bf16[256,2048]{1,0:T(8,128)(2,1)}, u32[]{:S(2)}, u32[]{:S(2)}) collective-permute-start(bf16[256,2048]{1,0:T(8,128)(2,1)} %collective-permute-done.2), channel_id=1, source_target_pairs={{0,1},{1,2},{2,3},{3,4},{4,5},{5,6},{6,7},{7,0},{8,9},{9,10},{10,1... | collective-permute-start | bytes 3145736 | tf_op jit(solution)/shard_map/ppermute | solution.py:38
  81.3 38.3 %all-to-all-start = ((bf16[2,64,2048]{2,0,1:T(2,128)(2,1)}), bf16[2,64,2048]{2,0,1:T(2,128)(2,1)S(1)}, u32[]{:S(2)}, u32[]{:S(2)}) async-start(bf16[2,64,2048]{2,0,1:T(2,128)(2,1)} %broadcast_select_fusion), calls=%async_computation | async-start | bytes 1048576 | tf_op jit(solution)/shard_map/all_to_all | solution.py:29
  119.8 27.3 %collective-permute-start.6 = (bf16[256,2048]{1,0:T(8,128)(2,1)}, bf16[256,2048]{1,0:T(8,128)(2,1)S(1)}, u32[]{:S(2)}, u32[]{:S(2)}) collective-permute-start(bf16[256,2048]{1,0:T(8,128)(2,1)} %collective-permute-done.5), channel_id=1, source_target_pairs={{0,7},{1,0},{2,1},{3,2},{4,3},{5,4},{6,5},{7,6},{8,15},{9,8},{10,9... | collective-permute-start | bytes 3145736 | tf_op jit(solution)/shard_map/ppermute | solution.py:40
